TPU v7x, 512 devices: a whole 4x8x8 slice. The times are simulated.
512 devices in a mesh: seq: 8 (over z), vocab: 64 (over y, x, core).
Axes of the slice: x: 4, y: 8, z: 8, core: 2. Of those that a mesh axis runs over, the one named last changes fastest.
Arguments:
- hidden: bfloat16 [2048, 8192], P('seq', 'vocab'), may hold values from -120 to 120
- head_weight: bfloat16 [8192, 98304], P('seq', 'vocab'), may hold values from -0.0625 to 0.0625
- vocab_basis: bfloat16 [98304, 1024], P('vocab', 'seq'), may hold values from -0.0048828125 to 0.0048828125
- keep_index: int32 [512], P('seq'), may hold values from 0 to 255, as said below
- counts: int32 [8], P('seq'), may hold values from 1 to 64, as said below
Outputs:
- coefficients: float32 [512, 1024], P('seq', 'vocab')
Inputs may be any that keep to these rules, and one draw needn't show every extreme that they name: `keep_index`: each owner's list is strictly increasing and ends at 255. `counts`: exactly one owner has all 64 slots live.
All inputs are finite; a program needn't handle non-finite values.
Results may differ from a plain program's by a relative error of at most 0.0032.
Values may be sent and summed in bfloat16 or wider, within the bound.
No kernel may reach another device: no remote copies, remote signals or barrier semaphores. Data moves between devices by JAX's collectives and lax.ppermute only.
A program may use at most 64 MiB of HBM per device.

v0:
```python
import jax
import jax.numpy as jnp
from jax import lax
from jax.sharding import PartitionSpec as P


def shards(hidden, head_weight, vocab_basis, keep_index, counts):
    chosen = jnp.take(hidden, keep_index, axis=0)
    features = lax.all_gather(chosen, "vocab", axis=1, tiled=True)
    pieces = lax.all_to_all(features, "seq", split_axis=1, concat_axis=0, tiled=True)
    owned = features.shape[0]
    logits = lax.psum_scatter(
        jnp.dot(pieces, head_weight, preferred_element_type=jnp.float32),
        "seq",
        scatter_dimension=0,
        tiled=True,
    )
    row_max = lax.pmax(jnp.max(logits, axis=1, keepdims=True), "vocab")
    weights = jnp.exp(logits - row_max)
    denominator, weighted = lax.psum(
        (jnp.sum(weights, axis=1, keepdims=True), jnp.sum(weights * logits, axis=1, keepdims=True)),
        "vocab",
    )
    expected = weighted / denominator
    centred = (logits - expected).astype(jnp.bfloat16)
    partial_sums = jnp.dot(
        centred,
        lax.all_gather(vocab_basis, "seq", axis=1, tiled=True),
        preferred_element_type=jnp.float32,
    )
    summed = lax.psum_scatter(partial_sums, "vocab", scatter_dimension=1, tiled=True)
    live_rows = jnp.arange(owned, dtype=jnp.int32) < counts[0]
    return jnp.where(live_rows[:, None], summed, jnp.float32(0.0))


def solution(mesh):
    in_specs = (P("seq", "vocab"), P("seq", "vocab"), P("vocab", "seq"), P("seq"), P("seq"))
    out_specs = P("seq", "vocab")
    return jax.shard_map(shards, mesh=mesh, in_specs=in_specs, out_specs=out_specs, check_vma=False)
```

profile of v0, /device:TPU:2, one launch (start us, length us, event | category | flops | bytes accessed | tf_op | source)
XLA Modules:
  0.0 629.6 jit_solution(8558448056872284931)
XLA Ops:
  6.5 0.8 compare_select_fusion
  7.3 0.8 compare_and_fusion
  8.2 1.5 gather_fusion
  9.6 0.7 broadcast_select_fusion
  10.3 0.0 all-gather.3.cloned.1.call-update
  10.3 0.0 reduce-scatter.2.cloned.1.call-start
  10.4 80.3 %all-gather.3.cloned.1.call-done = bf16[64,8192]{1,0:T(8,128)(2,1)} async-done(((bf16[64,128]{1,0:T(8,128)(2,1)}), bf16[64,8192]{1,0:T(8,128)(2,1)}) %all-gather.3.cloned.1.call-update) | async-done | bytes 1048592 | tf_op jit(solution)/shard_map/all_gather | solution.py:9
  90.7 1.3 copy.10
  92.0 36.3 %all_to_all.19 = bf16[64,8,1024]{2,0,1:T(8,128)(2,1)S(1)} all-to-all(bf16[64,8,1024]{2,0,1:T(8,128)(2,1)S(1)} %bitcast.17), channel_id=1, replica_groups=mesh['seq'=8,'vocab'=64] {'seq'}, dimensions={1} | all-to-all | bytes 2097152 | tf_op jit(solution)/shard_map/all_to_all | solution.py:10
  128.3 3.5 fusion.3
  131.8 0.0 reduce-scatter.2.cloned.1.call-update
  131.8 0.0 all-gather.5.cloned.1.call-start
  131.9 0.7 all-gather.5.cloned.1.call-update
  132.6 0.0 all-reduce.4.cloned.1.call-start
  132.6 43.5 %reduce-scatter.2.cloned.1.call-done = f32[64,1536]{1,0:T(8,128)} async-done(((f32[512,1536]{1,0:T(8,128)}), f32[64,1536]{1,0:T(8,128)}) %reduce-scatter.2.cloned.1.call-update) | async-done | bytes 393232 | tf_op jit(solution)/shard_map/reduce_scatter | solution.py:12
  176.1 1.1 reduce_max.9
  177.2 120.6 %pmax.7 = f32[64]{0:T(128)S(1)} all-reduce(f32[64]{0:T(128)S(1)} %reduce_max.9), channel_id=1, replica_groups=mesh['seq'=8,'vocab'=64] {'vocab'}, use_global_device_ids=true, to_apply=%region_2.3 | all-reduce | flops 64 | bytes 512 | tf_op jit(solution)/shard_map/pmax | solution.py:18
  297.8 1.2 fusion
  299.1 124.1 %all-reduce.1 = (f32[64,1]{0,1:T(1,128)S(1)}, f32[64,1]{0,1:T(1,128)S(1)}) all-reduce(f32[64,1]{0,1:T(1,128)S(1)} %bitcast.21, f32[64,1]{0,1:T(1,128)S(1)} %bitcast.20), channel_id=1, replica_groups=mesh['seq'=8,'vocab'=64] {'vocab'}, use_global_device_ids=true, to_apply=%region_4.5 | all-reduce | flops 128 | bytes 1024 | tf_op jit(solution)/shard_map/psum | solution.py:20
  423.2 4.2 fusion.1
  427.3 0.0 all-reduce.4.cloned.1.call-update
  428.0 1.3 dynamic-slice
  429.9 191.8 %all-reduce.4.cloned.1.call-done = f32[64,1024]{0,1:T(8,128)} async-done(((f32[64,1024]{0,1:T(8,128)}), f32[64,1024]{0,1:T(8,128)}) %all-reduce.4.cloned.1.call-update) | async-done | bytes 262160
  621.7 1.3 dynamic-slice_select_fusion
  (7 shorter events, 0.0 us)
Async XLA Ops:
  6.5 121.8 %copy-start = (bf16[1024,1536]{1,0:T(8,128)(2,1)S(1)}, bf16[1024,1536]{1,0:T(8,128)(2,1)}, u32[]{:S(2)}) copy-start(bf16[1024,1536]{1,0:T(8,128)(2,1)} %param.6) | copy-start | bytes 9437188
  6.5 84.1 %all-gather.3.cloned.1.call-start = ((), (), s32[]{:S(2)}) async-start(), calls=%async_computation.2 | async-start | bytes 1064960 | tf_op jit(solution)/shard_map/all_gather | solution.py:9
  10.3 165.7 %reduce-scatter.2.cloned.1.call-start = ((), (), s32[]{:S(2)}) async-start(), calls=%async_computation.3 | async-start | bytes 3538944 | tf_op jit(solution)/shard_map/reduce_scatter | solution.py:12
  131.8 291.3 %all-gather.5.cloned.1.call-start = ((), (), s32[]{:S(2)}) async-start(), calls=%async_computation.4 | async-start | bytes 3538944 | tf_op jit(solution)/shard_map/all_gather | solution.py:28
  132.6 489.2 %all-reduce.4.cloned.1.call-start = ((), (), s32[]{:S(2)}) async-start(), calls=%async_computation.5 | async-start | bytes 1048576
Sparse Core Ops, SparseCore 0:
  10.6 80.0 all-gather.2
  131.9 44.0 reduce-scatter.1
  178.1 57.3 all-gather.4
  427.5 194.2 all-reduce.3
where the time goes:
time: 630 us
  waiting for transfers between devices  316 us (50%)
  blocking collectives  281 us (45%)
  between operations  14.5 us (2%)
  matrix products  7.68 us (1%)
    unnamed x5, waiting for transfers between devices  193 us
    psum x1, blocking collectives, shards(): lax.psum((jnp.sum(weights, axis=1, keepdims=True), jnp.sum(weights * logi...  124 us
    pmax x1, blocking collectives, shards(): row_max = lax.pmax(jnp.max(logits, axis=1, keepdims=True), 'vocab')  121 us
    all_gather x1, waiting for transfers between devices, shards(): features = lax.all_gather(chosen, 'vocab', axis=1, tiled=True)  80.3 us
    reduce_scatter x1, waiting for transfers between devices, shards(): lax.psum_scatter(jnp.dot(pieces, head_weight, preferred_element_type=jnp....  43.5 us
    all_to_all x1, blocking collectives, shards(): lax.all_to_all(features, 'seq', split_axis=1, concat_axis=0, tiled=True)  36.3 us
  transfers between devices with their start and end apart: 4, of which 3 were waited for; matrix products, arithmetic and copies ran while one was open for 1% of the time, Pallas kernels for 0%

commit v1 on v0

--- a/solution.py
+++ b/solution.py
@@ -6,7 +6,9 @@
 
 def shards(hidden, head_weight, vocab_basis, keep_index, counts):
     chosen = jnp.take(hidden, keep_index, axis=0)
-    features = lax.all_gather(chosen, "vocab", axis=1, tiled=True)
+    features = jnp.concatenate(
+        lax.all_to_all(jnp.stack([chosen] * lax.axis_size("vocab")), "vocab", 0, 0), axis=1
+    )
     pieces = lax.all_to_all(features, "seq", split_axis=1, concat_axis=0, tiled=True)
     owned = features.shape[0]
     logits = lax.psum_scatter(

time: 630 us -> 593 us (0.941)
  waiting for transfers between devices: 316 us -> 235 us
  blocking collectives: 281 us -> 322 us
    all_gather x1 -> x0, waiting for transfers between devices: 80.3 us -> none  [shards(): features = lax.all_gather(chosen, 'vocab', axis=1, tiled=True)]
    all_to_all x0 -> x1, blocking collectives: none -> 39.2 us  [shards(): lax.all_to_all(jnp.stack([chosen] * lax.axis_size('vocab')), 'vocab', 0, 0)]
    unnamed x5 -> x4, waiting for transfers between devices: 193 us -> 193 us
  transfers between devices with their start and end apart: 4 -> 3, of which waited for: 3 -> 2; matrix products, arithmetic and copies ran while one was open for 1% -> 1% of each run, Pallas kernels for 0% -> 0%
where the time goes in v1:
time: 593 us; the launch traced here: 592 us
  blocking collectives  322 us (54%)
  waiting for transfers between devices  235 us (40%)
  between operations  14.4 us (2%)
  local copies, waits for them, and re-layouts  8.76 us (1%)
  matrix products  7.68 us (1%)
    unnamed x4, waiting for transfers between devices  193 us
    psum x1, blocking collectives, shards(): lax.psum((jnp.sum(weights, axis=1, keepdims=True), jnp.sum(weights * logi...  124 us
    pmax x1, blocking collectives, shards(): row_max = lax.pmax(jnp.max(logits, axis=1, keepdims=True), 'vocab')  120 us
    reduce_scatter x1, waiting for transfers between devices, shards(): lax.psum_scatter(jnp.dot(pieces, head_weight, preferred_element_type=jnp....  41.7 us
    all_to_all x1, blocking collectives, shards(): lax.all_to_all(jnp.stack([chosen] * lax.axis_size('vocab')), 'vocab', 0, 0)  39.2 us
    all_to_all x1, blocking collectives, shards(): lax.all_to_all(features, 'seq', split_axis=1, concat_axis=0, tiled=True)  37.9 us
  transfers between devices with their start and end apart: 3, of which 2 were waited for; matrix products, arithmetic and copies ran while one was open for 1% of the time, Pallas kernels for 0%

profile of v1, /device:TPU:2, one launch (start us, length us, event | category | flops | bytes accessed | tf_op | source)
XLA Modules:
  0.0 592.5 jit_solution(5772289169299730955)
XLA Ops:
  6.5 0.8 compare_select_fusion
  7.3 0.8 compare_and_fusion
  8.2 1.5 gather_fusion
  9.6 0.1 broadcast_select_fusion
  9.7 0.2 stack.2
  10.0 39.2 %all_to_all.24 = bf16[64,64,128]{2,1,0:T(8,128)(2,1)S(1)} all-to-all(bf16[64,64,128]{2,1,0:T(8,128)(2,1)S(1)} %stack.2), channel_id=1, replica_groups=mesh['seq'=8,'vocab'=64] {'vocab'}, dimensions={0} | all-to-all | bytes 2097152 | tf_op jit(solution)/shard_map/all_to_all | solution.py:10
  49.2 1.7 copy.7
  50.8 2.3 all_to_all.18
  53.1 1.8 copy.8
  55.0 37.9 %all_to_all.25 = bf16[64,8,1024]{2,0,1:T(8,128)(2,1)S(1)} all-to-all(bf16[64,8,1024]{2,0,1:T(8,128)(2,1)S(1)} %copy.8), channel_id=1, replica_groups=mesh['seq'=8,'vocab'=64] {'seq'}, dimensions={1} | all-to-all | bytes 2097152 | tf_op jit(solution)/shard_map/all_to_all | solution.py:12
  92.8 3.5 fusion.3
  96.3 0.0 reduce-scatter.2.cloned.1.call-update
  96.4 0.0 all-gather.2.cloned.1.call-start
  96.4 0.7 all-gather.2.cloned.1.call-update
  97.1 0.0 all-reduce.4.cloned.1.call-start
  97.2 41.7 %reduce-scatter.2.cloned.1.call-done = f32[64,1536]{1,0:T(8,128)} async-done(((f32[512,1536]{1,0:T(8,128)}), f32[64,1536]{1,0:T(8,128)}) %reduce-scatter.2.cloned.1.call-update) | async-done | bytes 393232 | tf_op jit(solution)/shard_map/reduce_scatter | solution.py:14
  138.9 1.1 reduce_max.9
  140.0 120.4 %pmax.7 = f32[64]{0:T(128)S(1)} all-reduce(f32[64]{0:T(128)S(1)} %reduce_max.9), channel_id=1, replica_groups=mesh['seq'=8,'vocab'=64] {'vocab'}, use_global_device_ids=true, to_apply=%region_2.3 | all-reduce | flops 64 | bytes 512 | tf_op jit(solution)/shard_map/pmax | solution.py:20
  260.5 1.2 fusion
  261.7 124.1 %all-reduce.1 = (f32[64,1]{0,1:T(1,128)S(1)}, f32[64,1]{0,1:T(1,128)S(1)}) all-reduce(f32[64,1]{0,1:T(1,128)S(1)} %bitcast.17, f32[64,1]{0,1:T(1,128)S(1)} %bitcast.16), channel_id=1, replica_groups=mesh['seq'=8,'vocab'=64] {'vocab'}, use_global_device_ids=true, to_apply=%region_4.5 | all-reduce | flops 128 | bytes 1024 | tf_op jit(solution)/shard_map/psum | solution.py:22
  385.8 4.2 fusion.1
  390.6 1.3 dynamic-slice
  392.6 192.1 %all-reduce.4.cloned.1.call-done = f32[64,1024]{0,1:T(8,128)} async-done(((f32[64,1024]{0,1:T(8,128)}), f32[64,1024]{0,1:T(8,128)}) %all-reduce.4.cloned.1.call-update) | async-done | bytes 262160
  584.6 1.3 dynamic-slice_select_fusion
  (8 shorter events, 0.0 us)
Async XLA Ops:
  6.5 86.3 %copy-start = (bf16[1024,1536]{1,0:T(8,128)(2,1)S(1)}, bf16[1024,1536]{1,0:T(8,128)(2,1)}, u32[]{:S(2)}) copy-start(bf16[1024,1536]{1,0:T(8,128)(2,1)} %param.6) | copy-start | bytes 9437188
  6.5 132.4 %reduce-scatter.2.cloned.1.call-start = ((), (), s32[]{:S(2)}) async-start(), calls=%async_computation.3 | async-start | bytes 3538944 | tf_op jit(solution)/shard_map/reduce_scatter | solution.py:14
  96.4 289.4 %all-gather.2.cloned.1.call-start = ((), (), s32[]{:S(2)}) async-start(), calls=%async_computation.4 | async-start | bytes 3538944 | tf_op jit(solution)/shard_map/all_gather | solution.py:30
  97.1 487.5 %all-reduce.4.cloned.1.call-start = ((), (), s32[]{:S(2)}) async-start(), calls=%async_computation.5 | async-start | bytes 1048576
Sparse Core Ops, SparseCore 0:
  96.5 42.3 reduce-scatter.1
  140.9 57.4 all-gather.1
  390.1 194.5 all-reduce.3
